TPU v7x, 256 devices: a whole 4x4x8 slice. The times are simulated.
256 devices in a mesh: task: 8 (over x_hi, y), mp: 32 (over x_lo, z, core).
Axes of the slice: x: 4 (x_hi: 2, x_lo: 2; x = x_hi * 2 + x_lo), y: 4, z: 8, core: 2. Of those that a mesh axis runs over, the one named last changes fastest.
Arguments:
- hidden: bfloat16 [8, 2048, 8192], P('task', 'mp'), may hold values from -6 to 6
- gain: float32 [8192], replicated, may hold values from 0.25 to 1.75
- tau: bfloat16 [8, 8192, 1024], P('task', 'mp'), may hold values from -0.0625 to 0.0625
- coeff: float32 [8, 8192, 1024], P('task', 'mp'), may hold values from 0.1 to 1
- counts: int32 [8], P('task'), may hold values from 683 to 2048, as said below
- positions: int32 [8, 2048], P('task', 'mp'), may hold values from 0 to 2047
Outputs:
- grad_coeff: float32 [8, 8192, 1024], P('task', 'mp')
- loss: float32 [], replicated
Inputs may be any that keep to these rules, and one draw needn't show every extreme that they name: `counts`: counts lie between a third of 2048 and 2048; some task has exactly 2048 in every draw. Rows at or past a task's count are not live.
All inputs are finite; a program needn't handle non-finite values.
Results may differ from a plain program's by a relative error of at most 0.0044.
The roundings to bfloat16 on the way count: a program that leaves them out, or rounds other values in their place, can miss the bound.
Values may be sent and summed in bfloat16 or wider, within the bound.
A program may use at most 64 MiB of HBM per device.

v0:
```python
import jax
import jax.numpy as jnp
from jax import lax
from jax.sharding import Mesh
from jax.sharding import PartitionSpec as P

HEAD = 128
MP = ("mp_0", "mp_1", "mp_2")
TASK = ("task_0", "task_1")
TASK_MP = ("task_0", "task_1", "mp_0", "mp_1", "mp_2")


def cut_along(value, dim, length):
    before, after = (value.shape[:dim], value.shape[dim + 1 :])
    return jnp.moveaxis(value.reshape(*before, length, -1, *after), dim, 0)


def scatter_pairs(value, chips, core, dim):
    sizes = (lax.axis_size(chips), lax.axis_size(core))
    tiles = cut_along(value, dim, sizes[0] * sizes[1])
    inside = tiles.shape[1:]
    tiles = tiles.reshape(*sizes, *inside).swapaxes(0, 1).reshape(-1, *inside)
    tiles = lax.psum_scatter(tiles, core, scatter_dimension=0, tiled=True)
    return lax.psum_scatter(tiles, chips, scatter_dimension=0, tiled=True)[0]


def by_axis(value, axes):
    for axis in axes:
        value = lax.psum(value, axis)
    return value


def rotary_tables(positions, head):
    index = jnp.arange(head // 2).astype(jnp.float32)
    freq = jnp.exp(-jnp.log(jnp.float32(1000000.0)) * 2.0 * index / head)
    angle = positions.astype(jnp.float32)[:, None] * freq[None, :]
    return (jnp.cos(angle), jnp.sin(angle))


def rotate(values, cosine, sine, sign, head):
    count = values.shape[0]
    width = values.shape[1]
    shaped = values.reshape(count, width // head, 2, head // 2)
    first = shaped[:, :, 0, :]
    second = shaped[:, :, 1, :]
    cosine = cosine[:, None, :]
    sine = sine[:, None, :] * sign
    out_first = first * cosine - second * sine
    out_second = second * cosine + first * sine
    return jnp.stack([out_first, out_second], axis=2).reshape(count, width)


def local(hidden, gain, tau, coeff, counts, positions):
    rows = hidden[0].astype(jnp.float32)
    width = rows.shape[1]
    keys = tau.shape[2]
    rows_local = rows.shape[0]
    inverse = 1.0 / jnp.sqrt(jnp.mean(rows * rows, axis=1, keepdims=True) + 1e-06)
    normed = (rows * inverse * gain[None, :]).astype(jnp.bfloat16)
    columns = lax.all_to_all(normed, MP, split_axis=1, concat_axis=0, tiled=True)
    tau_local = tau[0].astype(jnp.float32)
    mixed = lax.psum(coeff[0] * tau_local, TASK)
    merged = mixed.astype(jnp.bfloat16)
    teacher = tau[0]
    block = columns
    gap = scatter_pairs(
        jnp.dot(block, merged, preferred_element_type=jnp.float32)
        - jnp.dot(block, teacher, preferred_element_type=jnp.float32),
        ("mp_0", "mp_1"),
        "mp_2",
        0,
    )
    first_row = lax.axis_index(MP) * rows_local
    cosine, sine = rotary_tables(positions[0], HEAD)
    err = rotate(gap, cosine, sine, 1.0, HEAD)
    row_ids = first_row + jnp.arange(rows_local)
    live = (row_ids < counts[0]).astype(jnp.float32)[:, None]
    scale = 1.0 / (counts[0].astype(jnp.float32) * keys)
    partial_loss = jnp.sum(live * err * err) * scale
    back = rotate(2.0 * scale * live * err, cosine, sine, -1.0, HEAD).astype(jnp.bfloat16)
    block = columns
    local_grad = lax.dot_general(
        block,
        lax.all_gather(back, MP, axis=0, tiled=True),
        (((0,), (0,)), ((), ())),
        preferred_element_type=jnp.float32,
    )
    wgrad = lax.psum(local_grad, TASK)
    loss = by_axis(partial_loss, TASK_MP)
    grad_coeff = width * keys * tau_local * wgrad
    return (grad_coeff[None, :, :], loss)


def solution(mesh):
    split = Mesh(mesh.devices.reshape(2, 4, 2, 8, 2), ("task_0", "task_1", "mp_0", "mp_1", "mp_2"))
    placed = (P(TASK, MP, None), P(), P(TASK, MP, None), P(TASK, MP, None), P(TASK), P(TASK, MP))
    return jax.shard_map(
        local, mesh=split, in_specs=placed, out_specs=(P(TASK, MP, None), P()), check_vma=False
    )
```

profile of v0, /device:TPU:32, one launch (start us, length us, event | category | flops | bytes accessed | tf_op | source)
XLA Modules:
  0.0 391.9 jit_solution(13827501548182623606)
XLA Ops:
  7.2 1.5 multiply_reduce_fusion
  8.7 1.5 copy.13
  10.6 1.6 copy.11
  12.1 9.7 %all-to-all-start = ((bf16[64,32,256]{2,0,1:T(8,128)(2,1)}), bf16[64,32,256]{2,0,1:T(8,128)(2,1)S(1)}, u32[]{:S(2)}, u32[]{:S(2)}) async-start(bf16[64,32,256]{2,0,1:T(8,128)(2,1)} %copy.11), calls=%async_computation | async-start | bytes 2097152 | tf_op jit(solution)/shard_map/all_to_all | solution.py:60
  21.8 1.4 convert_multiply_fusion
  23.2 81.8 %all-reduce.4 = bf16[256,1024]{1,0:T(8,128)(2,1)S(1)} all-reduce(f32[256,1024]{1,0:T(8,128)S(1)} %convert_multiply_fusion), channel_id=1, replica_groups=mesh['task_0'=2,'task_1'=4,'mp_0'=2,'mp_1'=8,'mp_2'=2] {'task_0','task_1'}, use_global_device_ids=true, to_apply=%region_1.0 | all-reduce | flops 262144 | bytes 1572864 | tf_op jit(solution)/shard_map/psum | solution.py:62
  105.0 1.3 fusion.9
  106.3 1.3 convolution_subtract_fusion
  107.6 4.1 %copy.12 = f32[16,2,64,1024]{3,2,0,1:T(8,128)} copy(f32[16,2,64,1024]{3,2,1,0:T(8,128)S(1)} %bitcast.36) | data formatting | bytes 16777216 | tf_op jit(solution)/shard_map/reshape;reshape | solution.py:22
  111.7 19.8 %reduce-scatter.3.cloned.1.call-done = f32[16,64,1024]{2,1,0:T(8,128)} async-done(((f32[32,64,1024]{2,1,0:T(8,128)}), f32[16,64,1024]{2,1,0:T(8,128)}) %reduce-scatter.3.cloned.1.call-update) | async-done | bytes 4194320 | tf_op jit(solution)/shard_map/reduce_scatter | solution.py:23
  132.6 81.7 %reduce-scatter.5.cloned.1.call-done = f32[1,64,1024]{2,1,0:T(8,128)} async-done(((f32[16,64,1024]{2,1,0:T(8,128)}), f32[1,64,1024]{2,1,0:T(8,128)}) %reduce-scatter.5.cloned.1.call-update) | async-done | bytes 262160 | tf_op jit(solution)/shard_map/reduce_scatter | solution.py:24
  214.2 1.3 reshape_squeeze.3
  216.2 1.8 fusion.4
  218.6 0.7 pad_maximum_fusion.1
  219.3 0.9 convert_element_type.62
  220.3 64.3 %all-gather.2.cloned.1.call-done = bf16[2048,1024]{1,0:T(8,128)(2,1)} async-done(((bf16[64,1024]{1,0:T(8,128)(2,1)}), bf16[2048,1024]{1,0:T(8,128)(2,1)}) %all-gather.2.cloned.1.call-update) | async-done | bytes 4194320 | tf_op jit(solution)/shard_map/all_gather | solution.py:84
  284.5 4.4 %fusion.8 = f32[256,1024]{1,0:T(8,128)} fusion(bf16[2048,256]{1,0:T(8,128)(2,1)S(1)} %bitcast.40, bf16[2048,1024]{1,0:T(8,128)(2,1)} %all-gather.2.cloned.1.call-done), kind=kOutput, calls=%fused_computation.30 | convolution fusion | flops 1073741824 | bytes 6291456 | tf_op jit(solution)/shard_map/dot_general | solution.py:82
  289.6 6.9 %psum.51 = f32[]{:T(128)} all-reduce(f32[]{:T(128)S(6)} %mul.221), channel_id=1, replica_groups=mesh['task_0'=2,'task_1'=4,'mp_0'=2,'mp_1'=8,'mp_2'=2] {'task_0'}, use_global_device_ids=true, to_apply=%region_6.0 | all-reduce | flops 1 | bytes 8 | tf_op jit(solution)/shard_map/psum | solution.py:29
  296.6 11.5 %psum.52 = f32[]{:T(128)} all-reduce(f32[]{:T(128)} %psum.51), channel_id=1, replica_groups=mesh['task_0'=2,'task_1'=4,'mp_0'=2,'mp_1'=8,'mp_2'=2] {'task_1'}, use_global_device_ids=true, to_apply=%region_7.0 | all-reduce | flops 1 | bytes 8 | tf_op jit(solution)/shard_map/psum | solution.py:29
  308.1 5.5 %psum.53 = f32[]{:T(128)} all-reduce(f32[]{:T(128)} %psum.52), channel_id=1, replica_groups=mesh['task_0'=2,'task_1'=4,'mp_0'=2,'mp_1'=8,'mp_2'=2] {'mp_0'}, use_global_device_ids=true, to_apply=%region_8.0 | all-reduce | flops 1 | bytes 8 | tf_op jit(solution)/shard_map/psum | solution.py:29
  313.6 15.9 %psum.54 = f32[]{:T(128)} all-reduce(f32[]{:T(128)} %psum.53), channel_id=1, replica_groups=mesh['task_0'=2,'task_1'=4,'mp_0'=2,'mp_1'=8,'mp_2'=2] {'mp_1'}, use_global_device_ids=true, to_apply=%region_9.0 | all-reduce | flops 1 | bytes 8 | tf_op jit(solution)/shard_map/psum | solution.py:29
  329.5 3.1 psum.55
  332.5 50.5 %all-reduce.3.cloned.1.call-done = f32[256,1024]{1,0:T(8,128)} async-done(((f32[256,1024]{1,0:T(8,128)}), f32[256,1024]{1,0:T(8,128)}) %all-reduce.3.cloned.1.call-update) | async-done | bytes 1048592 | tf_op jit(solution)/shard_map/psum | solution.py:88
  383.0 2.4 fusion.3
  (25 shorter events, 2.0 us)
Async XLA Ops:
  7.2 3.1 copy-start.1
  10.2 11.6 %copy-start = (bf16[1,256,1024]{2,1,0:T(8,128)(2,1)S(1)}, bf16[1,256,1024]{2,1,0:T(8,128)(2,1)}, u32[]{:S(2)}) copy-start(bf16[1,256,1024]{2,1,0:T(8,128)(2,1)} %param.8) | copy-start | bytes 1572868
  12.1 92.9 %all-to-all-start = ((bf16[64,32,256]{2,0,1:T(8,128)(2,1)}), bf16[64,32,256]{2,0,1:T(8,128)(2,1)S(1)}, u32[]{:S(2)}, u32[]{:S(2)}) async-start(bf16[64,32,256]{2,0,1:T(8,128)(2,1)} %copy.11), calls=%async_computation | async-start | bytes 2097152 | tf_op jit(solution)/shard_map/all_to_all | solution.py:60
  21.8 109.8 %reduce-scatter.3.cloned.1.call-start = ((), (), s32[]{:S(2)}) async-start(), calls=%async_computation.3 | async-start | bytes 12582912 | tf_op jit(solution)/shard_map/reduce_scatter | solution.py:23
  111.7 20.7 %copy-start.2 = (s32[1,64]{1,0:T(1,128)S(1)}, s32[1,64]{1,0:T(1,128)}, u32[]{:S(2)}) copy-start(s32[1,64]{1,0:T(1,128)} %param.11) | copy-start | bytes 772
  111.7 102.6 %reduce-scatter.5.cloned.1.call-start = ((), (), s32[]{:S(2)}) async-start(), calls=%async_computation.4 | async-start | bytes 4456448 | tf_op jit(solution)/shard_map/reduce_scatter | solution.py:24
  131.6 153.0 %all-gather.2.cloned.1.call-start = ((), (), s32[]{:S(2)}) async-start(), calls=%async_computation.5 | async-start | bytes 4325376 | tf_op jit(solution)/shard_map/all_gather | solution.py:84
  220.2 162.8 %all-reduce.3.cloned.1.call-start = ((), (), s32[]{:S(2)}) async-start(), calls=%async_computation.6 | async-start | bytes 2097152 | tf_op jit(solution)/shard_map/psum | solution.py:88
Sparse Core Ops, SparseCore 0:
  111.8 19.7 reduce-scatter.2
  134.1 80.0 reduce-scatter.4
  220.3 64.1 all-gather.1
  289.1 93.8 all-reduce.2
where the time goes:
time: 392 us
  waiting for transfers between devices  216 us (55%)
  blocking collectives  125 us (32%)
  between operations  15.3 us (4%)
  starting transfers between devices  9.82 us (3%)
  other arithmetic  9.5 us (2%)
  local copies, waits for them, and re-layouts  9.36 us (2%)
  matrix products  6.95 us (2%)
    psum x1, blocking collectives, local(): mixed = lax.psum(coeff[0] * tau_local, TASK)  81.8 us
    reduce_scatter x1, waiting for transfers between devices, scatter_pairs(): return lax.psum_scatter(tiles, chips, scatter_dimension=0, tiled=True)[0]  81.7 us
    all_gather x1, waiting for transfers between devices, local(): lax.all_gather(back, MP, axis=0, tiled=True)  64.3 us
    psum x1, waiting for transfers between devices, local(): wgrad = lax.psum(local_grad, TASK)  50.5 us
    psum x5, blocking collectives, by_axis(): value = lax.psum(value, axis)  42.9 us
    reduce_scatter x1, waiting for transfers between devices, scatter_pairs(): tiles = lax.psum_scatter(tiles, core, scatter_dimension=0, tiled=True)  19.8 us
    all_to_all x1, starting transfers between devices, local(): lax.all_to_all(normed, MP, split_axis=1, concat_axis=0, tiled=True)  9.65 us
  transfers between devices with their start and end apart: 5, of which 4 were waited for; matrix products, arithmetic and copies ran while one was open for 0% of the time, Pallas kernels for 0%

commit v1 on v0

--- a/solution.py
+++ b/solution.py
@@ -85,7 +85,8 @@
         (((0,), (0,)), ((), ())),
         preferred_element_type=jnp.float32,
     )
-    wgrad = lax.psum(local_grad, TASK)
+    parts = lax.all_gather(local_grad, TASK)
+    wgrad = jnp.sum(parts, axis=0)
     loss = by_axis(partial_loss, TASK_MP)
     grad_coeff = width * keys * tau_local * wgrad
     return (grad_coeff[None, :, :], loss)

time: 392 us -> 415 us (1.059)
  waiting for transfers between devices: 216 us -> 235 us
    all_gather x0 -> x1, waiting for transfers between devices: none -> 69.1 us  [local(): parts = lax.all_gather(local_grad, TASK)]
    psum x1 -> x0, waiting for transfers between devices: 50.5 us -> none  [local(): wgrad = lax.psum(local_grad, TASK)]
    reduce_sum x0 -> x1, other arithmetic: none -> 4.38 us  [local(): wgrad = jnp.sum(parts, axis=0)]
where the time goes in v1:
time: 415 us; the launch traced here: 414 us
  waiting for transfers between devices  235 us (57%)
  blocking collectives  125 us (30%)
  between operations  15.3 us (4%)
  other arithmetic  12.8 us (3%)
  starting transfers between devices  9.82 us (2%)
  local copies, waits for them, and re-layouts  9.36 us (2%)
  matrix products  6.94 us (2%)
    reduce_scatter x1, waiting for transfers between devices, scatter_pairs(): return lax.psum_scatter(tiles, chips, scatter_dimension=0, tiled=True)[0]  82.1 us
    psum x1, blocking collectives, local(): mixed = lax.psum(coeff[0] * tau_local, TASK)  81.7 us
    all_gather x1, waiting for transfers between devices, local(): parts = lax.all_gather(local_grad, TASK)  69.1 us
    all_gather x1, waiting for transfers between devices, local(): lax.all_gather(back, MP, axis=0, tiled=True)  64 us
    psum x5, blocking collectives, by_axis(): value = lax.psum(value, axis)  43 us
    reduce_scatter x1, waiting for transfers between devices, scatter_pairs(): tiles = lax.psum_scatter(tiles, core, scatter_dimension=0, tiled=True)  19.9 us
    all_to_all x1, starting transfers between devices, local(): lax.all_to_all(normed, MP, split_axis=1, concat_axis=0, tiled=True)  9.65 us
  transfers between devices with their start and end apart: 5, of which 4 were waited for; matrix products, arithmetic and copies ran while one was open for 0% of the time, Pallas kernels for 0%

profile of v1, /device:TPU:32, one launch (start us, length us, event | category | flops | bytes accessed | tf_op | source)
XLA Modules:
  0.0 414.1 jit_solution(15596810838373076728)
XLA Ops:
  7.2 1.5 multiply_reduce_fusion
  8.7 1.5 copy.13
  10.5 1.6 copy.11
  12.1 9.7 %all-to-all-start = ((bf16[64,32,256]{2,0,1:T(8,128)(2,1)}), bf16[64,32,256]{2,0,1:T(8,128)(2,1)S(1)}, u32[]{:S(2)}, u32[]{:S(2)}) async-start(bf16[64,32,256]{2,0,1:T(8,128)(2,1)} %copy.11), calls=%async_computation | async-start | bytes 2097152 | tf_op jit(solution)/shard_map/all_to_all | solution.py:60
  21.8 1.5 bitcast_multiply_fusion.2
  23.3 81.7 %all-reduce.1 = bf16[256,1024]{1,0:T(8,128)(2,1)S(1)} all-reduce(f32[256,1024]{1,0:T(8,128)S(1)} %bitcast_multiply_fusion.2), channel_id=1, replica_groups=mesh['task_0'=2,'task_1'=4,'mp_0'=2,'mp_1'=8,'mp_2'=2] {'task_0','task_1'}, use_global_device_ids=true, to_apply=%region_1.0 | all-reduce | flops 262144 | bytes 1572864 | tf_op jit(solution)/shard_map/psum | solution.py:62
  105.1 1.3 fusion.7
  106.3 1.3 convolution_subtract_fusion
  107.6 4.1 copy.12
  111.7 19.9 %reduce-scatter.3.cloned.1.call-done = f32[16,64,1024]{2,1,0:T(8,128)} async-done(((f32[32,64,1024]{2,1,0:T(8,128)}), f32[16,64,1024]{2,1,0:T(8,128)}) %reduce-scatter.3.cloned.1.call-update) | async-done | bytes 4194320 | tf_op jit(solution)/shard_map/reduce_scatter | solution.py:23
  132.6 82.1 %reduce-scatter.5.cloned.1.call-done = f32[1,64,1024]{2,1,0:T(8,128)} async-done(((f32[16,64,1024]{2,1,0:T(8,128)}), f32[1,64,1024]{2,1,0:T(8,128)}) %reduce-scatter.5.cloned.1.call-update) | async-done | bytes 262160 | tf_op jit(solution)/shard_map/reduce_scatter | solution.py:24
  214.8 1.3 reshape_squeeze.3
  216.7 1.8 fusion.2
  219.9 0.9 convert_element_type.66
  220.8 64.0 %all-gather.4.cloned.1.call-done = bf16[2048,1024]{1,0:T(8,128)(2,1)} async-done(((bf16[64,1024]{1,0:T(8,128)(2,1)}), bf16[2048,1024]{1,0:T(8,128)(2,1)}) %all-gather.4.cloned.1.call-update) | async-done | bytes 4194320 | tf_op jit(solution)/shard_map/all_gather | solution.py:84
  284.8 4.4 %fusion.6 = f32[256,1024]{1,0:T(8,128)} fusion(bf16[2048,256]{1,0:T(8,128)(2,1)S(1)} %bitcast.40, bf16[2048,1024]{1,0:T(8,128)(2,1)} %all-gather.4.cloned.1.call-done), kind=kOutput, calls=%fused_computation.28 | convolution fusion | flops 1073741824 | bytes 6291456 | tf_op jit(solution)/shard_map/dot_general | solution.py:82
  289.9 6.9 %psum.43 = f32[]{:T(128)} all-reduce(f32[]{:T(128)S(6)} %mul.223), channel_id=1, replica_groups=mesh['task_0'=2,'task_1'=4,'mp_0'=2,'mp_1'=8,'mp_2'=2] {'task_0'}, use_global_device_ids=true, to_apply=%region_6.0 | all-reduce | flops 1 | bytes 8 | tf_op jit(solution)/shard_map/psum | solution.py:29
  296.8 11.1 %psum.44 = f32[]{:T(128)} all-reduce(f32[]{:T(128)} %psum.43), channel_id=1, replica_groups=mesh['task_0'=2,'task_1'=4,'mp_0'=2,'mp_1'=8,'mp_2'=2] {'task_1'}, use_global_device_ids=true, to_apply=%region_7.0 | all-reduce | flops 1 | bytes 8 | tf_op jit(solution)/shard_map/psum | solution.py:29
  307.9 5.8 %psum.45 = f32[]{:T(128)} all-reduce(f32[]{:T(128)} %psum.44), channel_id=1, replica_groups=mesh['task_0'=2,'task_1'=4,'mp_0'=2,'mp_1'=8,'mp_2'=2] {'mp_0'}, use_global_device_ids=true, to_apply=%region_8.0 | all-reduce | flops 1 | bytes 8 | tf_op jit(solution)/shard_map/psum | solution.py:29
  313.7 16.2 %psum.46 = f32[]{:T(128)} all-reduce(f32[]{:T(128)} %psum.45), channel_id=1, replica_groups=mesh['task_0'=2,'task_1'=4,'mp_0'=2,'mp_1'=8,'mp_2'=2] {'mp_1'}, use_global_device_ids=true, to_apply=%region_9.0 | all-reduce | flops 1 | bytes 8 | tf_op jit(solution)/shard_map/psum | solution.py:29
  329.8 3.1 psum.47
  332.9 69.1 %all-gather.6.cloned.1.call-done = f32[2048,1024]{1,0:T(8,128)} async-done(((f32[256,1024]{1,0:T(8,128)}), f32[2048,1024]{1,0:T(8,128)}) %all-gather.6.cloned.1.call-update) | async-done | bytes 8388624 | tf_op jit(solution)/shard_map/all_gather | solution.py:88
  402.0 4.4 %reduce_sum.30 = f32[256,1024]{1,0:T(8,128)S(1)} reduce(f32[8,256,1024]{2,1,0:T(8,128)} %bitcast.41, f32[]{:T(128)} %constant.16.clone.1), dimensions={0}, to_apply=%region_4.0 | reduce | flops 1835008 | bytes 9437188 | tf_op jit(solution)/shard_map/reduce_sum | solution.py:89
  406.4 1.2 bitcast_multiply_fusion.1
  (26 shorter events, 2.7 us)
Async XLA Ops:
  7.2 3.1 copy-start.1
  12.1 92.9 %all-to-all-start = ((bf16[64,32,256]{2,0,1:T(8,128)(2,1)}), bf16[64,32,256]{2,0,1:T(8,128)(2,1)S(1)}, u32[]{:S(2)}, u32[]{:S(2)}) async-start(bf16[64,32,256]{2,0,1:T(8,128)(2,1)} %copy.11), calls=%async_computation | async-start | bytes 2097152 | tf_op jit(solution)/shard_map/all_to_all | solution.py:60
  21.8 109.8 %reduce-scatter.3.cloned.1.call-start = ((), (), s32[]{:S(2)}) async-start(), calls=%async_computation.3 | async-start | bytes 12582912 | tf_op jit(solution)/shard_map/reduce_scatter | solution.py:23
  105.0 1.3 copy-start
  111.7 20.7 %copy-start.2 = (s32[1,64]{1,0:T(1,128)S(1)}, s32[1,64]{1,0:T(1,128)}, u32[]{:S(2)}) copy-start(s32[1,64]{1,0:T(1,128)} %param.11) | copy-start | bytes 772
  111.7 103.1 %reduce-scatter.5.cloned.1.call-start = ((), (), s32[]{:S(2)}) async-start(), calls=%async_computation.4 | async-start | bytes 4456448 | tf_op jit(solution)/shard_map/reduce_scatter | solution.py:24
  131.6 153.2 %all-gather.4.cloned.1.call-start = ((), (), s32[]{:S(2)}) async-start(), calls=%async_computation.5 | async-start | bytes 4325376 | tf_op jit(solution)/shard_map/all_gather | solution.py:84
  220.7 181.3 %all-gather.6.cloned.1.call-start = ((), (), s32[]{:S(2)}) async-start(), calls=%async_computation.6 | async-start | bytes 9437184 | tf_op jit(solution)/shard_map/all_gather | solution.py:88
Sparse Core Ops, SparseCore 0:
  111.8 19.7 reduce-scatter.2
  134.1 80.5 reduce-scatter.4
  220.9 63.8 all-gather.3
  289.4 112.6 all-gather.5
